TPU v7x, 256 devices: a whole 4x4x8 slice. The times are simulated.
256 devices in a mesh: dp: 8 (over z), seq: 32 (over x, y, core).
Axes of the slice: x: 4, y: 4, z: 8, core: 2. Of those that a mesh axis runs over, the one named last changes fastest.
Arguments:
- seq_in: bfloat16 [65536, 1536], P(('dp', 'seq')), parts along dimension 0, may hold values from -6 to 6
- conv_gain: float32 [1536], replicated, may hold values from 0.1 to 1.9
- convolution_weight: bfloat16 [3, 1536, 768], replicated, may hold values from -0.09375 to 0.09375
- conv_bias: float32 [768], replicated, may hold values from -3 to 3
- attn_gain: float32 [1536], replicated, may hold values from 0.1 to 1.9
- w_query: bfloat16 [1536, 512], replicated
- w_key: bfloat16 [1536, 128], replicated
- w_value: bfloat16 [1536, 128], replicated, may hold values from -0.15625 to 0.15625
- w_out: bfloat16 [512, 1536], replicated, may hold values from -0.25 to 0.25
Outputs:
- block_out: bfloat16 [65536, 1536], P(('dp', 'seq')), parts along dimension 0
There are 8 independent parts, one for each index of `dp`. A program takes and returns all parts, laid end to end along the dimension named above; an argument that names none is the same for every part. Nothing has to cross between parts.
All inputs are finite; a program needn't handle non-finite values.
Results may differ from a plain program's by a relative error of at most 0.0059.
Values may be sent and summed in bfloat16 or wider, within the bound.
A program may use at most 128 MiB of HBM per device.

v0:
```python
import jax
import jax.numpy as jnp
from jax import lax
from jax.sharding import PartitionSpec as P

DILATION_STEP = 4


def padded(cells, sides, width):
    for axis, dim in sides:
        count = lax.axis_size(axis)
        ends = count - 1
        head = lax.slice_in_dim(cells, 0, width, axis=dim)
        tail = lax.slice_in_dim(cells, cells.shape[dim] - width, cells.shape[dim], axis=dim)
        cells = jnp.concatenate(
            [
                lax.ppermute(tail, axis, [(i, (i + 1) % count) for i in range(ends)]),
                cells,
                lax.ppermute(head, axis, [((i + 1) % count, i) for i in range(ends)]),
            ],
            axis=dim,
        )
    return cells


def normalize(values, gain_vec):
    wide = values.astype(jnp.float32)
    meansq = jnp.mean(wide * wide, axis=-1, keepdims=True)
    return wide * lax.rsqrt(meansq + 1e-06) * gain_vec


def fold_block(state_now, keys_vals, queries, head_dim):
    maxima, totals, summed = state_now
    key_part = keys_vals[:, :head_dim]
    value_part = keys_vals[:, head_dim:]
    scores = jnp.einsum(
        "thd,kd->htk", queries, key_part, preferred_element_type=jnp.float32
    ) * head_dim ** (-0.5)
    new_max = jnp.maximum(maxima, jnp.max(scores, axis=-1))
    factor = jnp.exp(maxima - new_max)
    expd = jnp.exp(scores - new_max[..., None])
    totals = totals * factor + jnp.sum(expd, axis=-1)
    summed = summed * factor[..., None] + jnp.einsum(
        "htk,kd->htd", expd.astype(jnp.bfloat16), value_part, preferred_element_type=jnp.float32
    )
    return (new_max, totals, summed)


def body(
    seq_in, conv_gain, convolution_weight, conv_bias, attn_gain, w_query, w_key, w_value, w_out
):
    token_rows = seq_in.shape[0]
    kernel_taps = convolution_weight.shape[0]
    head_dim = w_key.shape[1]
    heads_all = w_query.shape[1] // head_dim
    out_chan = convolution_weight.shape[2]
    receptive_reach = DILATION_STEP * (kernel_taps - 1) // 2
    normed = normalize(seq_in, conv_gain).astype(jnp.bfloat16)
    padded_tokens = padded(normed, (("seq", 0),), receptive_reach)
    convolved_total = jnp.dot(
        padded_tokens[0:token_rows], convolution_weight[0], preferred_element_type=jnp.float32
    )
    for tap_index in range(1, kernel_taps):
        convolved_total = convolved_total + jnp.dot(
            padded_tokens[tap_index * DILATION_STEP : tap_index * DILATION_STEP + token_rows],
            convolution_weight[tap_index],
            preferred_element_type=jnp.float32,
        )
    activated = jax.nn.gelu(convolved_total + conv_bias, approximate=True)
    wide_in = seq_in.astype(jnp.float32)
    hidden = jnp.concatenate(
        [wide_in[:, :out_chan] + activated, wide_in[:, out_chan:]], axis=1
    ).astype(jnp.bfloat16)
    attn_in = normalize(hidden, attn_gain).astype(jnp.bfloat16)
    queries = jnp.dot(attn_in, w_query, preferred_element_type=jnp.float32).astype(jnp.bfloat16)
    queries = queries.reshape(token_rows, heads_all, head_dim)
    key_rows = jnp.dot(attn_in, w_key, preferred_element_type=jnp.float32).astype(jnp.bfloat16)
    value_rows = jnp.dot(attn_in, w_value, preferred_element_type=jnp.float32).astype(jnp.bfloat16)
    packed = jnp.concatenate([key_rows, value_rows], axis=1)
    start_state = (
        jnp.full((heads_all, token_rows), -1e30, jnp.float32),
        jnp.zeros((heads_all, token_rows), jnp.float32),
        jnp.zeros((heads_all, token_rows, head_dim), jnp.float32),
    )
    gathered = lax.all_gather(packed, "seq", axis=0, tiled=True)
    shards = lax.axis_size("seq")
    group = 1
    for g in range(1, shards + 1):
        if shards % g == 0 and g * token_rows <= 2048:
            group = g
    span = token_rows * group
    count = gathered.shape[0] // span

    def step_keys(block_index, state_now):
        block_rows = lax.dynamic_slice_in_dim(gathered, block_index * span, span, 0)
        return fold_block(state_now, block_rows, queries, head_dim)

    final_state = lax.fori_loop(0, count, step_keys, start_state)
    maxima, totals, summed = final_state
    result = summed / totals[..., None]
    attended = (
        jnp.transpose(result, (1, 0, 2))
        .reshape(token_rows, heads_all * head_dim)
        .astype(jnp.bfloat16)
    )
    mixed = hidden.astype(jnp.float32) + jnp.dot(
        attended, w_out, preferred_element_type=jnp.float32
    )
    return mixed.astype(jnp.bfloat16)


def solution(mesh):
    placed = (P(("dp", "seq"), None), P(), P(), P(), P(), P(), P(), P(), P())
    return jax.shard_map(
        body, mesh=mesh, in_specs=placed, out_specs=P(("dp", "seq"), None), check_vma=False
    )
```

profile of v0, /device:TPU:1, one launch (start us, length us, event | category | flops | bytes accessed | tf_op | source)
XLA Modules:
  0.0 116.0 jit_solution(7414915342071189569)
XLA Ops:
  6.5 1.5 %multiply_reduce_fusion = f32[256]{0:T(256)S(1)} fusion(bf16[256,1536]{1,0:T(8,128)(2,1)} %param.11), kind=kLoop, calls=%fused_computation.34 | loop fusion | flops 1179392 | bytes 787456 | tf_op jit(solution)/shard_map/reduce_sum | solution.py:28
  8.0 1.4 %multiply_convert_fusion = bf16[256,1536]{1,0:T(8,128)(2,1)S(1)} fusion(f32[1536]{0:T(1024)} %param.12, f32[256]{0:T(256)S(1)} %add_rsqrt_fusion.1, bf16[256,1536]{1,0:T(8,128)(2,1)} %param.11), kind=kLoop, calls=%fused_computation.33 | loop fusion | flops 1572864 | bytes 1580032 | tf_op jit(solution)/shard_map/convert_element_type | solution.py:58
  9.5 4.6 %collective-permute-start = (bf16[4,1536]{1,0:T(4,128)(2,1)S(1)}, bf16[4,1536]{1,0:T(4,128)(2,1)S(1)}, u32[]{:S(2)}, u32[]{:S(2)}) collective-permute-start(bf16[4,1536]{1,0:T(4,128)(2,1)S(1)} %get-tuple-element.166), channel_id=1, source_target_pairs={{0,1},{1,2},{2,3},{3,4},{4,5},{5,6},{6,7},{7,8},{8,9},{9,10},{10,1... | collective-permute-start | bytes 36872 | tf_op jit(solution)/shard_map/ppermute | solution.py:17
  14.1 2.1 %collective-permute-start.1 = (bf16[4,1536]{1,0:T(4,128)(2,1)S(1)}, bf16[4,1536]{1,0:T(4,128)(2,1)S(1)}, u32[]{:S(2)}, u32[]{:S(2)}) collective-permute-start(bf16[4,1536]{1,0:T(4,128)(2,1)S(1)} %get-tuple-element.167), channel_id=1, source_target_pairs={{1,0},{2,1},{3,2},{4,3},{5,4},{6,5},{7,6},{8,7},{9,8},{10,9},{11,1... | collective-permute-start | bytes 36872 | tf_op jit(solution)/shard_map/ppermute | solution.py:19
  16.1 2.6 %fusion.15 = f32[256,768]{1,0:T(8,128)S(1)} fusion(bf16[256,1536]{1,0:T(8,128)(2,1)S(1)} %multiply_convert_fusion, bf16[3,1536,768]{2,1,0:T(8,128)(2,1)} %param.13), kind=kOutput, calls=%fused_computation.23 | convolution fusion | flops 603979776 | bytes 3932160 | tf_op jit(solution)/shard_map/dot_general | solution.py:64
  18.8 0.2 convert_element_type.43
  19.0 0.2 collective-permute-done.1
  19.2 0.6 copy-done.2
  19.8 0.8 fusion.13
  20.7 1.0 fusion.47
  21.7 0.2 fusion.22
  22.0 0.5 convolution_convert_fusion.1
  22.5 0.2 copy-done.4
  22.7 0.5 convolution_convert_fusion.2
  23.2 0.7 pad_maximum_fusion.5
  23.9 2.0 %fusion.34 = bf16[32,4,8,128]{3,2,1,0:T(8,128)(2,1)S(1)} fusion(bf16[1536,512]{1,0:T(8,128)(2,1)} %param.16, f32[1536]{0:T(1024)S(1)} %copy-done.5, f32[256]{0:T(256)S(1)} %add_rsqrt_fusion, bf16[256,768]{1,0:T(8,128)(2,1)S(1)} %slice.52, bf16[256,768]{1,0:T(8,128)(2,1)S(1)} %fusion.47), kind=kOutput, calls=%fused_computation.40 | convolution fusion | flops 405536768 | bytes 2628608 | tf_op jit(solution)/shard_map/dot_general | solution.py:75
  26.0 55.1 %all-gather.2.cloned.1.call-done = bf16[8192,256]{0,1:T(8,128)(2,1)} async-done(((bf16[256,256]{0,1:T(8,128)(2,1)}), bf16[8192,256]{0,1:T(8,128)(2,1)}) %all-gather.2.cloned.1.call-update) | async-done | bytes 4194320 | tf_op jit(solution)/shard_map/all_gather | solution.py:85
  81.1 26.3 %while.18 = (s32[]{:T(128)}, f32[4,256]{1,0:T(4,128)S(1)}, f32[4,256]{1,0:T(4,128)S(1)}, f32[4,256,128]{2,1,0:T(8,128)S(1)}, bf16[8192,256]{0,1:T(8,128)(2,1)}, ...) while((s32[]{:T(128)}, f32[4,256]{1,0:T(4,128)S(1)}, ...), condition=%wide.region_5.0_spmd.clone, body=%wide.region_2.0_spmd.clone.sunk | while | flops 1090917376 | bytes 27590852 | solution.py:98
  81.1 2.3 %bitcast_reduce_fusion.2 = (f32[4,256]{1,0:T(4,128)S(1)}, f32[2048,256,4]{1,0,2:T(8,128)S(1)}) fusion(bf16[256,4,128]{2,0,1:T(8,128)(2,1)S(1)} %get-tuple-element.240, bf16[8192,256]{0,1:T(8,128)(2,1)} %get-tuple-element.239, s32[]{:T(128)S(6)} %select_n.9), kind=kOutput, calls=%fused_computation.1.clone.1 | convolution fusion | flops 541064192 | bytes 9179140 | tf_op jit(solution)/shard_map/while/body/eval_jaxpr/thd,kd->htk/dot_general | solution.py:36
  83.4 1.4 %fusion.72 = f32[4,256]{1,0:T(4,128)S(1)} fusion(f32[2048,256,4]{1,0,2:T(8,128)S(1)} %get-tuple-element.210, f32[4,256]{1,0:T(4,128)S(1)} %select_maximum_fusion.2), kind=kLoop, calls=%fused_computation.4.clone.1 | loop fusion | flops 6290432 | bytes 8396800 | tf_op jit(solution)/shard_map/while/body/eval_jaxpr/reduce_sum | solution.py:42
  84.8 2.8 %fusion.74 = f32[4,256,128]{2,1,0:T(8,128)S(1)} fusion(f32[2048,256,4]{1,0,2:T(8,128)S(1)} %get-tuple-element.210, f32[4,256]{1,0:T(4,128)S(1)} %select_maximum_fusion.2, bf16[8192,256]{0,1:T(8,128)(2,1)} %get-tuple-element.239, s32[]{:T(128)S(6)} %select_n.9, s32[]{:T(128)S(6)} %add.170, f32[4,256,128]{2,1,0:T(8,128)S(1)} %get-tuple-element.227, ...), kind=kOutput, calls=%fused_computation.6.clone.1 | convolution fusion | flops 543555584 | bytes 9969673 | tf_op jit(solution)/shard_map/while/body/eval_jaxpr/htk,kd->htd/dot_general | solution.py:43
  87.7 2.4 %bitcast_reduce_fusion.2 = (f32[4,256]{1,0:T(4,128)S(1)}, f32[2048,256,4]{1,0,2:T(8,128)S(1)}) fusion(bf16[256,4,128]{2,0,1:T(8,128)(2,1)S(1)} %get-tuple-element.240, bf16[8192,256]{0,1:T(8,128)(2,1)} %get-tuple-element.239, s32[]{:T(128)S(6)} %select_n.9), kind=kOutput, calls=%fused_computation.1.clone.1 | convolution fusion | flops 541064192 | bytes 9179140 | tf_op jit(solution)/shard_map/while/body/eval_jaxpr/thd,kd->htk/dot_general | solution.py:36
  90.0 1.4 %fusion.72 = f32[4,256]{1,0:T(4,128)S(1)} fusion(f32[2048,256,4]{1,0,2:T(8,128)S(1)} %get-tuple-element.210, f32[4,256]{1,0:T(4,128)S(1)} %select_maximum_fusion.2), kind=kLoop, calls=%fused_computation.4.clone.1 | loop fusion | flops 6290432 | bytes 8396800 | tf_op jit(solution)/shard_map/while/body/eval_jaxpr/reduce_sum | solution.py:42
  91.4 2.8 %fusion.74 = f32[4,256,128]{2,1,0:T(8,128)S(1)} fusion(f32[2048,256,4]{1,0,2:T(8,128)S(1)} %get-tuple-element.210, f32[4,256]{1,0:T(4,128)S(1)} %select_maximum_fusion.2, bf16[8192,256]{0,1:T(8,128)(2,1)} %get-tuple-element.239, s32[]{:T(128)S(6)} %select_n.9, s32[]{:T(128)S(6)} %add.170, f32[4,256,128]{2,1,0:T(8,128)S(1)} %get-tuple-element.227, ...), kind=kOutput, calls=%fused_computation.6.clone.1 | convolution fusion | flops 543555584 | bytes 9969673 | tf_op jit(solution)/shard_map/while/body/eval_jaxpr/htk,kd->htd/dot_general | solution.py:43
  94.3 2.4 %bitcast_reduce_fusion.2 = (f32[4,256]{1,0:T(4,128)S(1)}, f32[2048,256,4]{1,0,2:T(8,128)S(1)}) fusion(bf16[256,4,128]{2,0,1:T(8,128)(2,1)S(1)} %get-tuple-element.240, bf16[8192,256]{0,1:T(8,128)(2,1)} %get-tuple-element.239, s32[]{:T(128)S(6)} %select_n.9), kind=kOutput, calls=%fused_computation.1.clone.1 | convolution fusion | flops 541064192 | bytes 9179140 | tf_op jit(solution)/shard_map/while/body/eval_jaxpr/thd,kd->htk/dot_general | solution.py:36
  96.6 1.4 %fusion.72 = f32[4,256]{1,0:T(4,128)S(1)} fusion(f32[2048,256,4]{1,0,2:T(8,128)S(1)} %get-tuple-element.210, f32[4,256]{1,0:T(4,128)S(1)} %select_maximum_fusion.2), kind=kLoop, calls=%fused_computation.4.clone.1 | loop fusion | flops 6290432 | bytes 8396800 | tf_op jit(solution)/shard_map/while/body/eval_jaxpr/reduce_sum | solution.py:42
  98.0 2.8 %fusion.74 = f32[4,256,128]{2,1,0:T(8,128)S(1)} fusion(f32[2048,256,4]{1,0,2:T(8,128)S(1)} %get-tuple-element.210, f32[4,256]{1,0:T(4,128)S(1)} %select_maximum_fusion.2, bf16[8192,256]{0,1:T(8,128)(2,1)} %get-tuple-element.239, s32[]{:T(128)S(6)} %select_n.9, s32[]{:T(128)S(6)} %add.170, f32[4,256,128]{2,1,0:T(8,128)S(1)} %get-tuple-element.227, ...), kind=kOutput, calls=%fused_computation.6.clone.1 | convolution fusion | flops 543555584 | bytes 9969673 | tf_op jit(solution)/shard_map/while/body/eval_jaxpr/htk,kd->htd/dot_general | solution.py:43
  100.8 2.4 %bitcast_reduce_fusion.2 = (f32[4,256]{1,0:T(4,128)S(1)}, f32[2048,256,4]{1,0,2:T(8,128)S(1)}) fusion(bf16[256,4,128]{2,0,1:T(8,128)(2,1)S(1)} %get-tuple-element.240, bf16[8192,256]{0,1:T(8,128)(2,1)} %get-tuple-element.239, s32[]{:T(128)S(6)} %select_n.9), kind=kOutput, calls=%fused_computation.1.clone.1 | convolution fusion | flops 541064192 | bytes 9179140 | tf_op jit(solution)/shard_map/while/body/eval_jaxpr/thd,kd->htk/dot_general | solution.py:36
  103.2 1.4 %fusion.72 = f32[4,256]{1,0:T(4,128)S(1)} fusion(f32[2048,256,4]{1,0,2:T(8,128)S(1)} %get-tuple-element.210, f32[4,256]{1,0:T(4,128)S(1)} %select_maximum_fusion.2), kind=kLoop, calls=%fused_computation.4.clone.1 | loop fusion | flops 6290432 | bytes 8396800 | tf_op jit(solution)/shard_map/while/body/eval_jaxpr/reduce_sum | solution.py:42
  104.6 2.8 %fusion.74 = f32[4,256,128]{2,1,0:T(8,128)S(1)} fusion(f32[2048,256,4]{1,0,2:T(8,128)S(1)} %get-tuple-element.210, f32[4,256]{1,0:T(4,128)S(1)} %select_maximum_fusion.2, bf16[8192,256]{0,1:T(8,128)(2,1)} %get-tuple-element.239, s32[]{:T(128)S(6)} %select_n.9, s32[]{:T(128)S(6)} %add.170, f32[4,256,128]{2,1,0:T(8,128)S(1)} %get-tuple-element.227, ...), kind=kOutput, calls=%fused_computation.6.clone.1 | convolution fusion | flops 543555584 | bytes 9969673 | tf_op jit(solution)/shard_map/while/body/eval_jaxpr/htk,kd->htd/dot_general | solution.py:43
  107.4 0.2 copy.16
  107.7 1.5 %fusion.12 = bf16[256,1536]{1,0:T(8,128)(2,1)} fusion(bf16[256,512]{0,1:T(8,128)(2,1)S(1)} %bitcast.71, bf16[512,1536]{1,0:T(8,128)(2,1)S(1)} %copy-done, bf16[256,768]{1,0:T(8,128)(2,1)S(1)} %slice.52, bf16[256,768]{1,0:T(8,128)(2,1)S(1)} %fusion.47), kind=kOutput, calls=%fused_computation.18 | convolution fusion | flops 405012480 | bytes 3407872 | tf_op jit(solution)/shard_map/dot_general | solution.py:106
  (36 shorter events, 0.3 us)
Async XLA Ops:
  6.5 101.2 %copy-start = (bf16[512,1536]{1,0:T(8,128)(2,1)S(1)}, bf16[512,1536]{1,0:T(8,128)(2,1)}, u32[]{:S(2)}) copy-start(bf16[512,1536]{1,0:T(8,128)(2,1)} %param.19) | copy-start | bytes 4718596
  6.5 74.5 %all-gather.2.cloned.1.call-start = ((), (), s32[]{:S(2)}) async-start(), calls=%async_computation | async-start | bytes 4325376 | tf_op jit(solution)/shard_map/all_gather | solution.py:85
  9.5 11.2 %collective-permute-start = (bf16[4,1536]{1,0:T(4,128)(2,1)S(1)}, bf16[4,1536]{1,0:T(4,128)(2,1)S(1)}, u32[]{:S(2)}, u32[]{:S(2)}) collective-permute-start(bf16[4,1536]{1,0:T(4,128)(2,1)S(1)} %get-tuple-element.166), channel_id=1, source_target_pairs={{0,1},{1,2},{2,3},{3,4},{4,5},{5,6},{6,7},{7,8},{8,9},{9,10},{10,1... | collective-permute-start | bytes 36872 | tf_op jit(solution)/shard_map/ppermute | solution.py:17
  14.1 4.7 %copy-start.1 = (bf16[256,1536]{1,0:T(8,128)(2,1)S(1)}, bf16[256,1536]{1,0:T(8,128)(2,1)}, u32[]{:S(2)}) copy-start(bf16[256,1536]{1,0:T(8,128)(2,1)} %param.11) | copy-start | bytes 2359300
  14.1 5.1 %collective-permute-start.1 = (bf16[4,1536]{1,0:T(4,128)(2,1)S(1)}, bf16[4,1536]{1,0:T(4,128)(2,1)S(1)}, u32[]{:S(2)}, u32[]{:S(2)}) collective-permute-start(bf16[4,1536]{1,0:T(4,128)(2,1)S(1)} %get-tuple-element.167), channel_id=1, source_target_pairs={{1,0},{2,1},{3,2},{4,3},{5,4},{6,5},{7,6},{8,7},{9,8},{10,9},{11,1... | collective-permute-start | bytes 36872 | tf_op jit(solution)/shard_map/ppermute | solution.py:19
  16.1 3.7 %copy-start.2 = (bf16[3,1536,768]{2,1,0:T(8,128)(2,1)S(1)}, bf16[3,1536,768]{2,1,0:T(8,128)(2,1)}, u32[]{:S(2)}) copy-start(bf16[3,1536,768]{2,1,0:T(8,128)(2,1)} %param.13) | copy-start | bytes 21233668
  19.0 1.7 %copy-start.6 = (f32[768]{0:T(1024)S(1)}, f32[768]{0:T(1024)}, u32[]{:S(2)}) copy-start(f32[768]{0:T(1024)} %param.14) | copy-start | bytes 9220
  20.6 1.3 %copy-start.3 = (bf16[1536,128]{1,0:T(8,128)(2,1)S(1)}, bf16[1536,128]{1,0:T(8,128)(2,1)}, u32[]{:S(2)}) copy-start(bf16[1536,128]{1,0:T(8,128)(2,1)} %param.18) | copy-start | bytes 1179652
  20.7 1.3 %copy-start.5 = (f32[1536]{0:T(1024)S(1)}, f32[1536]{0:T(1024)}, u32[]{:S(2)}) copy-start(f32[1536]{0:T(1024)} %param.15) | copy-start | bytes 18436
  21.7 1.0 copy-start.4
Sparse Core Ops, SparseCore 0:
  24.0 57.0 all-gather.1
where the time goes:
time: 117 us; the launch traced here: 116 us
  waiting for transfers between devices  55.3 us (47%)
  matrix products  29.4 us (25%)
  between operations  13.6 us (12%)
  other arithmetic  9.62 us (8%)
  starting transfers between devices  6.64 us (6%)
  local copies, waits for them, and re-layouts  1.19 us (1%)
    all_gather x1, waiting for transfers between devices, body(): gathered = lax.all_gather(packed, 'seq', axis=0, tiled=True)  55.1 us
    dot_general x4, matrix products, fold_block(): jnp.einsum('htk,kd->htd', expd.astype(jnp.bfloat16), value_part, preferre...  11.2 us
    dot_general x4, matrix products, fold_block(): jnp.einsum('thd,kd->htk', queries, key_part, preferred_element_type=jnp.f...  9.4 us
    reduce_sum x4, other arithmetic, fold_block(): totals = totals * factor + jnp.sum(expd, axis=-1)  5.49 us
    ppermute x1, starting transfers between devices, padded(): lax.ppermute(tail, axis, [(i, (i + 1) % count) for i in range(ends)])  4.58 us
    dot_general x2, matrix products, body(): jnp.dot(padded_tokens[tap_index * DILATION_STEP:tap_index * DILATION_STEP...  3.38 us
  transfers between devices with their start and end apart: 3, of which 2 were waited for; matrix products, arithmetic and copies ran while one was open for 5% of the time, Pallas kernels for 0%

commit v1 on v0

--- a/solution.py
+++ b/solution.py
@@ -82,7 +82,9 @@
         jnp.zeros((heads_all, token_rows), jnp.float32),
         jnp.zeros((heads_all, token_rows, head_dim), jnp.float32),
     )
-    gathered = lax.all_gather(packed, "seq", axis=0, tiled=True)
+    gathered = jnp.concatenate(
+        lax.all_to_all(jnp.stack([packed] * lax.axis_size("seq")), "seq", 0, 0), axis=0
+    )
     shards = lax.axis_size("seq")
     group = 1
     for g in range(1, shards + 1):

time: 117 us -> 108 us (0.923)
  between operations: 13.6 us -> 0.27 us
  starting transfers between devices: 6.64 us -> 14.5 us
  waiting for transfers between devices: 55.3 us -> 50.2 us
  local copies, waits for them, and re-layouts: 1.19 us -> 3.75 us
    all_gather x1 -> x0, waiting for transfers between devices: 55.1 us -> none  [body(): gathered = lax.all_gather(packed, 'seq', axis=0, tiled=True)]
    all_to_all x0 -> x1, waiting for transfers between devices: none -> 50 us  [body(): lax.all_to_all(jnp.stack([packed] * lax.axis_size('seq')), 'seq', 0, 0)]
    all_to_all x0 -> x1, starting transfers between devices: none -> 7.83 us  [body(): lax.all_to_all(jnp.stack([packed] * lax.axis_size('seq')), 'seq', 0, 0)]
    another operation x0 -> x1, local copies, waits for them, and re-layouts: none -> 2.44 us  [body(): jnp.stack([packed] * lax.axis_size('seq'))]
where the time goes in v1:
time: 108 us; the launch traced here: 107 us
  waiting for transfers between devices  50.2 us (46%)
  matrix products  29.1 us (27%)
  starting transfers between devices  14.5 us (13%)
  other arithmetic  8.97 us (8%)
  local copies, waits for them, and re-layouts  3.75 us (3%)
    all_to_all x1, waiting for transfers between devices, body(): lax.all_to_all(jnp.stack([packed] * lax.axis_size('seq')), 'seq', 0, 0)  50 us
    dot_general x4, matrix products, fold_block(): jnp.einsum('htk,kd->htd', expd.astype(jnp.bfloat16), value_part, preferre...  11.1 us
    dot_general x4, matrix products, fold_block(): jnp.einsum('thd,kd->htk', queries, key_part, preferred_element_type=jnp.f...  9.23 us
    all_to_all x1, starting transfers between devices, body(): lax.all_to_all(jnp.stack([packed] * lax.axis_size('seq')), 'seq', 0, 0)  7.83 us
    reduce_sum x4, other arithmetic, fold_block(): totals = totals * factor + jnp.sum(expd, axis=-1)  5.49 us
    ppermute x1, starting transfers between devices, padded(): lax.ppermute(tail, axis, [(i, (i + 1) % count) for i in range(ends)])  4.58 us
    dot_general x2, matrix products, body(): jnp.dot(padded_tokens[tap_index * DILATION_STEP:tap_index * DILATION_STEP...  3.39 us
    another operation x1, local copies, waits for them, and re-layouts, body(): jnp.stack([packed] * lax.axis_size('seq'))  2.44 us
  transfers between devices with their start and end apart: 3, of which 2 were waited for; matrix products, arithmetic and copies ran while one was open for 5% of the time, Pallas kernels for 0%

profile of v1, /device:TPU:1, one launch (start us, length us, event | category | flops | bytes accessed | tf_op | source)
XLA Modules:
  0.0 107.0 jit_solution(13897760712812418780)
XLA Ops:
  0.0 1.5 %multiply_reduce_fusion = f32[256]{0:T(256)S(1)} fusion(bf16[256,1536]{1,0:T(8,128)(2,1)} %param.11), kind=kLoop, calls=%fused_computation.34 | loop fusion | flops 1179392 | bytes 787456 | tf_op jit(solution)/shard_map/reduce_sum | solution.py:28
  1.5 1.4 %multiply_convert_fusion = bf16[256,1536]{1,0:T(8,128)(2,1)S(1)} fusion(f32[1536]{0:T(1024)} %param.12, f32[256]{0:T(256)S(1)} %add_rsqrt_fusion.1, bf16[256,1536]{1,0:T(8,128)(2,1)} %param.11), kind=kLoop, calls=%fused_computation.33 | loop fusion | flops 1572864 | bytes 1580032 | tf_op jit(solution)/shard_map/convert_element_type | solution.py:58
  2.9 4.6 %collective-permute-start = (bf16[4,1536]{1,0:T(4,128)(2,1)S(1)}, bf16[4,1536]{1,0:T(4,128)(2,1)S(1)}, u32[]{:S(2)}, u32[]{:S(2)}) collective-permute-start(bf16[4,1536]{1,0:T(4,128)(2,1)S(1)} %get-tuple-element.166), channel_id=1, source_target_pairs={{0,1},{1,2},{2,3},{3,4},{4,5},{5,6},{6,7},{7,8},{8,9},{9,10},{10,1... | collective-permute-start | bytes 36872 | tf_op jit(solution)/shard_map/ppermute | solution.py:17
  7.5 2.1 %collective-permute-start.1 = (bf16[4,1536]{1,0:T(4,128)(2,1)S(1)}, bf16[4,1536]{1,0:T(4,128)(2,1)S(1)}, u32[]{:S(2)}, u32[]{:S(2)}) collective-permute-start(bf16[4,1536]{1,0:T(4,128)(2,1)S(1)} %get-tuple-element.167), channel_id=1, source_target_pairs={{1,0},{2,1},{3,2},{4,3},{5,4},{6,5},{7,6},{8,7},{9,8},{10,9},{11,1... | collective-permute-start | bytes 36872 | tf_op jit(solution)/shard_map/ppermute | solution.py:19
  9.6 2.6 %fusion.15 = f32[256,768]{1,0:T(8,128)S(1)} fusion(bf16[256,1536]{1,0:T(8,128)(2,1)S(1)} %multiply_convert_fusion, bf16[3,1536,768]{2,1,0:T(8,128)(2,1)} %param.13), kind=kOutput, calls=%fused_computation.23 | convolution fusion | flops 603979776 | bytes 3932160 | tf_op jit(solution)/shard_map/dot_general | solution.py:64
  12.4 0.2 collective-permute-done.1
  12.7 0.6 copy-done.2
  13.3 0.8 fusion.13
  14.2 1.0 fusion.47
  15.2 0.2 fusion.22
  15.4 0.5 convolution_convert_fusion.1
  15.9 0.2 copy-done.4
  16.2 0.5 convolution_convert_fusion.2
  16.8 2.4 %stack.2 = bf16[32,256,256]{2,1,0:T(8,128)(2,1)} broadcast(bf16[256,256]{1,0:T(8,128)(2,1)S(1)} %copy.14), dimensions={1,2} | broadcast | bytes 4325376 | tf_op jit(solution)/shard_map/stack | solution.py:86
  19.2 7.8 %all-to-all-start = ((bf16[32,256,256]{2,1,0:T(8,128)(2,1)}), bf16[32,256,256]{2,1,0:T(8,128)(2,1)}, u32[]{:S(2)}, u32[]{:S(2)}) async-start(bf16[32,256,256]{2,1,0:T(8,128)(2,1)} %stack.2), calls=%async_computation | async-start | bytes 8388608 | tf_op jit(solution)/shard_map/all_to_all | solution.py:86
  27.1 2.0 %fusion.34 = bf16[32,4,8,128]{3,2,1,0:T(8,128)(2,1)S(1)} fusion(bf16[1536,512]{1,0:T(8,128)(2,1)} %param.16, f32[1536]{0:T(1024)S(1)} %copy-done.5, f32[256]{0:T(256)S(1)} %add_rsqrt_fusion, bf16[256,768]{1,0:T(8,128)(2,1)S(1)} %slice.52, bf16[256,768]{1,0:T(8,128)(2,1)S(1)} %fusion.47), kind=kOutput, calls=%fused_computation.40 | convolution fusion | flops 405536768 | bytes 2628608 | tf_op jit(solution)/shard_map/dot_general | solution.py:75
  29.2 50.0 %all-to-all-done = bf16[32,256,256]{2,1,0:T(8,128)(2,1)} async-done(((bf16[32,256,256]{2,1,0:T(8,128)(2,1)}), bf16[32,256,256]{2,1,0:T(8,128)(2,1)}, u32[]{:S(2)}, u32[]{:S(2)}) %all-to-all-start) | async-done | bytes 4194336 | tf_op jit(solution)/shard_map/all_to_all | solution.py:86
  79.2 26.0 %while.18 = (s32[]{:T(128)}, f32[4,256]{1,0:T(4,128)S(1)}, f32[4,256]{1,0:T(4,128)S(1)}, f32[4,256,128]{2,1,0:T(8,128)S(1)}, bf16[8192,256]{1,0:T(8,128)(2,1)}, ...) while((s32[]{:T(128)}, f32[4,256]{1,0:T(4,128)S(1)}, ...), condition=%wide.region_5.0_spmd.clone, body=%wide.region_2.0_spmd.clone.sunk | while | flops 1090917376 | bytes 27590852 | solution.py:100
  79.2 2.3 %bitcast_reduce_fusion.2 = (f32[4,256]{1,0:T(4,128)S(1)}, f32[2048,256,4]{1,0,2:T(8,128)S(1)}) fusion(bf16[256,4,128]{2,0,1:T(8,128)(2,1)S(1)} %get-tuple-element.240, bf16[8192,256]{1,0:T(8,128)(2,1)} %get-tuple-element.239, s32[]{:T(128)S(6)} %select_n.9), kind=kOutput, calls=%fused_computation.1.clone.1 | convolution fusion | flops 541064192 | bytes 9179140 | tf_op jit(solution)/shard_map/while/body/eval_jaxpr/thd,kd->htk/dot_general | solution.py:36
  81.5 1.4 %fusion.72 = f32[4,256]{1,0:T(4,128)S(1)} fusion(f32[2048,256,4]{1,0,2:T(8,128)S(1)} %get-tuple-element.210, f32[4,256]{1,0:T(4,128)S(1)} %select_maximum_fusion.2), kind=kLoop, calls=%fused_computation.4.clone.1 | loop fusion | flops 6290432 | bytes 8396800 | tf_op jit(solution)/shard_map/while/body/eval_jaxpr/reduce_sum | solution.py:42
  82.9 2.8 %fusion.74 = f32[4,256,128]{2,1,0:T(8,128)S(1)} fusion(f32[2048,256,4]{1,0,2:T(8,128)S(1)} %get-tuple-element.210, f32[4,256]{1,0:T(4,128)S(1)} %select_maximum_fusion.2, bf16[8192,256]{1,0:T(8,128)(2,1)} %get-tuple-element.239, s32[]{:T(128)S(6)} %select_n.9, s32[]{:T(128)S(6)} %add.170, f32[4,256,128]{2,1,0:T(8,128)S(1)} %get-tuple-element.227, ...), kind=kOutput, calls=%fused_computation.6.clone.1 | convolution fusion | flops 543555584 | bytes 9969673 | tf_op jit(solution)/shard_map/while/body/eval_jaxpr/htk,kd->htd/dot_general | solution.py:43
  85.7 2.3 %bitcast_reduce_fusion.2 = (f32[4,256]{1,0:T(4,128)S(1)}, f32[2048,256,4]{1,0,2:T(8,128)S(1)}) fusion(bf16[256,4,128]{2,0,1:T(8,128)(2,1)S(1)} %get-tuple-element.240, bf16[8192,256]{1,0:T(8,128)(2,1)} %get-tuple-element.239, s32[]{:T(128)S(6)} %select_n.9), kind=kOutput, calls=%fused_computation.1.clone.1 | convolution fusion | flops 541064192 | bytes 9179140 | tf_op jit(solution)/shard_map/while/body/eval_jaxpr/thd,kd->htk/dot_general | solution.py:36
  88.0 1.4 %fusion.72 = f32[4,256]{1,0:T(4,128)S(1)} fusion(f32[2048,256,4]{1,0,2:T(8,128)S(1)} %get-tuple-element.210, f32[4,256]{1,0:T(4,128)S(1)} %select_maximum_fusion.2), kind=kLoop, calls=%fused_computation.4.clone.1 | loop fusion | flops 6290432 | bytes 8396800 | tf_op jit(solution)/shard_map/while/body/eval_jaxpr/reduce_sum | solution.py:42
  89.4 2.8 %fusion.74 = f32[4,256,128]{2,1,0:T(8,128)S(1)} fusion(f32[2048,256,4]{1,0,2:T(8,128)S(1)} %get-tuple-element.210, f32[4,256]{1,0:T(4,128)S(1)} %select_maximum_fusion.2, bf16[8192,256]{1,0:T(8,128)(2,1)} %get-tuple-element.239, s32[]{:T(128)S(6)} %select_n.9, s32[]{:T(128)S(6)} %add.170, f32[4,256,128]{2,1,0:T(8,128)S(1)} %get-tuple-element.227, ...), kind=kOutput, calls=%fused_computation.6.clone.1 | convolution fusion | flops 543555584 | bytes 9969673 | tf_op jit(solution)/shard_map/while/body/eval_jaxpr/htk,kd->htd/dot_general | solution.py:43
  92.2 2.3 %bitcast_reduce_fusion.2 = (f32[4,256]{1,0:T(4,128)S(1)}, f32[2048,256,4]{1,0,2:T(8,128)S(1)}) fusion(bf16[256,4,128]{2,0,1:T(8,128)(2,1)S(1)} %get-tuple-element.240, bf16[8192,256]{1,0:T(8,128)(2,1)} %get-tuple-element.239, s32[]{:T(128)S(6)} %select_n.9), kind=kOutput, calls=%fused_computation.1.clone.1 | convolution fusion | flops 541064192 | bytes 9179140 | tf_op jit(solution)/shard_map/while/body/eval_jaxpr/thd,kd->htk/dot_general | solution.py:36
  94.5 1.4 %fusion.72 = f32[4,256]{1,0:T(4,128)S(1)} fusion(f32[2048,256,4]{1,0,2:T(8,128)S(1)} %get-tuple-element.210, f32[4,256]{1,0:T(4,128)S(1)} %select_maximum_fusion.2), kind=kLoop, calls=%fused_computation.4.clone.1 | loop fusion | flops 6290432 | bytes 8396800 | tf_op jit(solution)/shard_map/while/body/eval_jaxpr/reduce_sum | solution.py:42
  95.9 2.8 %fusion.74 = f32[4,256,128]{2,1,0:T(8,128)S(1)} fusion(f32[2048,256,4]{1,0,2:T(8,128)S(1)} %get-tuple-element.210, f32[4,256]{1,0:T(4,128)S(1)} %select_maximum_fusion.2, bf16[8192,256]{1,0:T(8,128)(2,1)} %get-tuple-element.239, s32[]{:T(128)S(6)} %select_n.9, s32[]{:T(128)S(6)} %add.170, f32[4,256,128]{2,1,0:T(8,128)S(1)} %get-tuple-element.227, ...), kind=kOutput, calls=%fused_computation.6.clone.1 | convolution fusion | flops 543555584 | bytes 9969673 | tf_op jit(solution)/shard_map/while/body/eval_jaxpr/htk,kd->htd/dot_general | solution.py:43
  98.7 2.3 %bitcast_reduce_fusion.2 = (f32[4,256]{1,0:T(4,128)S(1)}, f32[2048,256,4]{1,0,2:T(8,128)S(1)}) fusion(bf16[256,4,128]{2,0,1:T(8,128)(2,1)S(1)} %get-tuple-element.240, bf16[8192,256]{1,0:T(8,128)(2,1)} %get-tuple-element.239, s32[]{:T(128)S(6)} %select_n.9), kind=kOutput, calls=%fused_computation.1.clone.1 | convolution fusion | flops 541064192 | bytes 9179140 | tf_op jit(solution)/shard_map/while/body/eval_jaxpr/thd,kd->htk/dot_general | solution.py:36
  101.0 1.4 %fusion.72 = f32[4,256]{1,0:T(4,128)S(1)} fusion(f32[2048,256,4]{1,0,2:T(8,128)S(1)} %get-tuple-element.210, f32[4,256]{1,0:T(4,128)S(1)} %select_maximum_fusion.2), kind=kLoop, calls=%fused_computation.4.clone.1 | loop fusion | flops 6290432 | bytes 8396800 | tf_op jit(solution)/shard_map/while/body/eval_jaxpr/reduce_sum | solution.py:42
  102.4 2.8 %fusion.74 = f32[4,256,128]{2,1,0:T(8,128)S(1)} fusion(f32[2048,256,4]{1,0,2:T(8,128)S(1)} %get-tuple-element.210, f32[4,256]{1,0:T(4,128)S(1)} %select_maximum_fusion.2, bf16[8192,256]{1,0:T(8,128)(2,1)} %get-tuple-element.239, s32[]{:T(128)S(6)} %select_n.9, s32[]{:T(128)S(6)} %add.170, f32[4,256,128]{2,1,0:T(8,128)S(1)} %get-tuple-element.227, ...), kind=kOutput, calls=%fused_computation.6.clone.1 | convolution fusion | flops 543555584 | bytes 9969673 | tf_op jit(solution)/shard_map/while/body/eval_jaxpr/htk,kd->htd/dot_general | solution.py:43
  105.2 0.2 copy.16
  105.5 1.5 %fusion.12 = bf16[256,1536]{1,0:T(8,128)(2,1)} fusion(bf16[256,512]{0,1:T(8,128)(2,1)S(1)} %bitcast.70, bf16[512,1536]{1,0:T(8,128)(2,1)S(1)} %copy-done, bf16[256,768]{1,0:T(8,128)(2,1)S(1)} %slice.52, bf16[256,768]{1,0:T(8,128)(2,1)S(1)} %fusion.47), kind=kOutput, calls=%fused_computation.18 | convolution fusion | flops 405012480 | bytes 3407872 | tf_op jit(solution)/shard_map/dot_general | solution.py:108
  (37 shorter events, 0.6 us)
Async XLA Ops:
  0.0 105.5 %copy-start = (bf16[512,1536]{1,0:T(8,128)(2,1)S(1)}, bf16[512,1536]{1,0:T(8,128)(2,1)}, u32[]{:S(2)}) copy-start(bf16[512,1536]{1,0:T(8,128)(2,1)} %param.19) | copy-start | bytes 4718596
  2.9 11.2 %collective-permute-start = (bf16[4,1536]{1,0:T(4,128)(2,1)S(1)}, bf16[4,1536]{1,0:T(4,128)(2,1)S(1)}, u32[]{:S(2)}, u32[]{:S(2)}) collective-permute-start(bf16[4,1536]{1,0:T(4,128)(2,1)S(1)} %get-tuple-element.166), channel_id=1, source_target_pairs={{0,1},{1,2},{2,3},{3,4},{4,5},{5,6},{6,7},{7,8},{8,9},{9,10},{10,1... | collective-permute-start | bytes 36872 | tf_op jit(solution)/shard_map/ppermute | solution.py:17
  7.5 4.7 %copy-start.1 = (bf16[256,1536]{1,0:T(8,128)(2,1)S(1)}, bf16[256,1536]{1,0:T(8,128)(2,1)}, u32[]{:S(2)}) copy-start(bf16[256,1536]{1,0:T(8,128)(2,1)} %param.11) | copy-start | bytes 2359300
  7.5 5.1 %collective-permute-start.1 = (bf16[4,1536]{1,0:T(4,128)(2,1)S(1)}, bf16[4,1536]{1,0:T(4,128)(2,1)S(1)}, u32[]{:S(2)}, u32[]{:S(2)}) collective-permute-start(bf16[4,1536]{1,0:T(4,128)(2,1)S(1)} %get-tuple-element.167), channel_id=1, source_target_pairs={{1,0},{2,1},{3,2},{4,3},{5,4},{6,5},{7,6},{8,7},{9,8},{10,9},{11,1... | collective-permute-start | bytes 36872 | tf_op jit(solution)/shard_map/ppermute | solution.py:19
  9.6 3.7 %copy-start.2 = (bf16[3,1536,768]{2,1,0:T(8,128)(2,1)S(1)}, bf16[3,1536,768]{2,1,0:T(8,128)(2,1)}, u32[]{:S(2)}) copy-start(bf16[3,1536,768]{2,1,0:T(8,128)(2,1)} %param.13) | copy-start | bytes 21233668
  12.4 1.7 %copy-start.6 = (f32[768]{0:T(1024)S(1)}, f32[768]{0:T(1024)}, u32[]{:S(2)}) copy-start(f32[768]{0:T(1024)} %param.14) | copy-start | bytes 9220
  14.1 1.3 %copy-start.3 = (bf16[1536,128]{1,0:T(8,128)(2,1)S(1)}, bf16[1536,128]{1,0:T(8,128)(2,1)}, u32[]{:S(2)}) copy-start(bf16[1536,128]{1,0:T(8,128)(2,1)} %param.18) | copy-start | bytes 1179652
  14.1 1.3 %copy-start.5 = (f32[1536]{0:T(1024)S(1)}, f32[1536]{0:T(1024)}, u32[]{:S(2)}) copy-start(f32[1536]{0:T(1024)} %param.15) | copy-start | bytes 18436
  15.2 1.0 copy-start.4
  19.2 60.0 %all-to-all-start = ((bf16[32,256,256]{2,1,0:T(8,128)(2,1)}), bf16[32,256,256]{2,1,0:T(8,128)(2,1)}, u32[]{:S(2)}, u32[]{:S(2)}) async-start(bf16[32,256,256]{2,1,0:T(8,128)(2,1)} %stack.2), calls=%async_computation | async-start | bytes 8388608 | tf_op jit(solution)/shard_map/all_to_all | solution.py:86
